TPU v7x, 32 devices: a whole 2x2x4 slice. The times are simulated.
32 devices in a mesh: seq: 8 (over z, x), head: 4 (over y, core).
Axes of the slice: x: 2, y: 2, z: 4, core: 2. Of those that a mesh axis runs over, the one named last changes fastest.
Arguments:
- hidden_in: bfloat16 [256, 4096], P(None, 'seq'), may hold values from -6 to 6
- norm_gain: bfloat16 [1, 4096], P(None, 'seq'), may hold values from 0.25 to 1.75
- w_query: bfloat16 [4096, 4096], P('seq', 'head'), may hold values from -1 to 1
- w_key: bfloat16 [4096, 1024], P('seq', 'head'), may hold values from -1 to 1
- w_value: bfloat16 [4096, 1024], P('seq', 'head'), may hold values from -0.09375 to 0.09375
- w_out: bfloat16 [4096, 4096], P('head', 'seq'), may hold values from -0.09375 to 0.09375
- cache_keys: bfloat16 [32768, 8, 128], P('seq', 'head'), may hold values from -400 to 400
- cache_values: bfloat16 [32768, 8, 128], P('seq', 'head'), may hold values from -12 to 12
- lengths: int32 [8], replicated, may hold values from 512 to 4096, as said below
- span_start: int32 [1], replicated, may hold values from 0 to 256
Outputs:
- attn_out: bfloat16 [256, 4096], P('head', 'seq')
Inputs may be any that keep to these rules, and one draw needn't show every extreme that they name: Slots 0 to lengths[s] - 1 of shard s are live, the others empty; in every draw some shard is full.
All inputs are finite; a program needn't handle non-finite values.
Results may differ from a plain program's by a relative error of at most 0.039.
The roundings to bfloat16 on the way count: a program that leaves them out, or rounds other values in their place, can miss the bound.
Values may be sent and summed in bfloat16 or wider, within the bound.
No kernel may reach another device: no remote copies, remote signals or barrier semaphores. Data moves between devices by JAX's collectives and lax.ppermute only.
A program may use at most 64 MiB of HBM per device.

v0:
```python
import math
import jax
import jax.numpy as jnp
from jax import lax
from jax.sharding import PartitionSpec as P

D = 4096
rope_base = 500000.0
stretch = 64.0
initial_context = 8192.0
ramp_low = 1.0
ramp_high = 32.0
epsilon = 1e-05
negative = -1e30


def rope_parts(positions, head_dim):
    half_dim = head_dim // 2
    indices = jnp.arange(half_dim, dtype=jnp.float32)
    base_freq = jnp.power(jnp.float32(rope_base), -2.0 * indices / head_dim)
    wavelength = 2.0 * math.pi / base_freq
    turn_count = initial_context / wavelength
    ramp_share = jnp.clip((turn_count - ramp_low) / (ramp_high - ramp_low), 0.0, 1.0)
    frequency = (1.0 - ramp_share) * base_freq / stretch + ramp_share * base_freq
    angles = positions[:, None] * frequency[None, :]
    mscale = 0.1 * math.log(stretch) + 1.0
    return (jnp.cos(angles) * mscale, jnp.sin(angles) * mscale)


def rotate(vectors, cosine, sine_part):
    half_dim = vectors.shape[-1] // 2
    lower_half = vectors[..., :half_dim]
    upper_half = vectors[..., half_dim:]
    cosine = cosine[:, None, :]
    sine_part = sine_part[:, None, :]
    return jnp.concatenate(
        [
            lower_half * cosine - upper_half * sine_part,
            upper_half * cosine + lower_half * sine_part,
        ],
        -1,
    )


def round_trip(values):
    return lax.optimization_barrier(values.astype(jnp.bfloat16)).astype(jnp.float32)


def attend(running, queries, key_block, value_block, visible):
    maxima, totals, weighted = running
    scores = jnp.einsum("tgrd,kgd->grtk", queries, key_block, preferred_element_type=jnp.float32)
    scores = jnp.where(visible, scores, negative)
    new_max = jnp.maximum(maxima, jnp.max(scores, axis=-1))
    probability = jnp.where(visible, jnp.exp(scores - new_max[..., None]), 0.0)
    rescale = jnp.exp(maxima - new_max)
    totals = totals * rescale + jnp.sum(probability, axis=-1)
    weighted = weighted * rescale[..., None] + jnp.einsum(
        "grtk,kgd->grtd",
        probability.astype(jnp.bfloat16),
        value_block,
        preferred_element_type=jnp.float32,
    )
    return (new_max, totals, weighted)


def local(
    hidden_in,
    norm_gain,
    w_query,
    w_key,
    w_value,
    w_out,
    cache_keys,
    cache_values,
    lengths,
    span_start,
):
    seq_count = lax.axis_size("seq")
    my_index = lax.axis_index("seq")
    span_len = hidden_in.shape[0]
    local_kv = cache_keys.shape[1]
    head_dim = cache_keys.shape[2]
    group_size = w_query.shape[1] // (local_kv * head_dim)
    kv_cols = w_key.shape[1]
    row_count = span_len // seq_count
    first_new = my_index * row_count
    input_f32 = hidden_in.astype(jnp.float32)
    square_sums = lax.psum(jnp.sum(input_f32 * input_f32, axis=1), "seq")
    inv_rms = lax.rsqrt(square_sums[:, None] / D + epsilon)
    normed = (input_f32 * inv_rms * norm_gain.astype(jnp.float32)).astype(jnp.bfloat16)
    queries = lax.psum(jnp.dot(normed, w_query, preferred_element_type=jnp.float32), "seq")
    kv_own = lax.psum_scatter(
        jnp.concatenate(
            [
                jnp.dot(normed, w_key, preferred_element_type=jnp.float32),
                jnp.dot(normed, w_value, preferred_element_type=jnp.float32),
            ],
            1,
        ),
        "seq",
        scatter_dimension=0,
        tiled=True,
    )
    key_own = kv_own[:, :kv_cols]
    value_own = kv_own[:, kv_cols:]
    shard_ids = jnp.arange(lengths.shape[0], dtype=jnp.int32)
    offset = jnp.sum(jnp.where(shard_ids < my_index, lengths, 0))
    live_count = jnp.sum(jnp.where(shard_ids == my_index, lengths, 0))
    first_pos = jnp.sum(lengths) + span_start[0]
    query_pos = (first_pos + jnp.arange(span_len, dtype=jnp.int32)).astype(jnp.float32)
    cosine, sine_part = rope_parts(query_pos, head_dim)
    rotated = rotate(
        queries.reshape(span_len, local_kv * group_size, head_dim), cosine, sine_part
    ) * head_dim ** (-0.5)
    query_low = rotated.astype(jnp.bfloat16).reshape(span_len, local_kv, group_size, head_dim)
    my_keys = round_trip(key_own).reshape(row_count, local_kv, head_dim)
    my_values = value_own.astype(jnp.bfloat16).reshape(row_count, local_kv, head_dim)
    new_pos = (first_pos + first_new + jnp.arange(row_count, dtype=jnp.int32)).astype(jnp.float32)
    new_cos, new_sin = rope_parts(new_pos, head_dim)
    new_key_rot = rotate(my_keys, new_cos, new_sin).astype(jnp.bfloat16)
    block_len = math.gcd(cache_keys.shape[0], 1024)

    def sweep_block(block_index, running):
        block_start = block_index * block_len
        key_block = lax.dynamic_slice_in_dim(cache_keys, block_start, block_len, 0).astype(
            jnp.float32
        )
        value_block = lax.dynamic_slice_in_dim(cache_values, block_start, block_len, 0)
        slot_ids = block_start + jnp.arange(block_len, dtype=jnp.int32)
        occupied = slot_ids < live_count
        positions = (offset + slot_ids).astype(jnp.float32)
        block_cos, block_sin = rope_parts(positions, head_dim)
        block_keys = rotate(key_block, block_cos, block_sin).astype(jnp.bfloat16)
        return attend(running, query_low, block_keys, value_block, occupied[None, None, None, :])

    running = (
        jnp.full((local_kv, group_size, span_len), negative, jnp.float32),
        jnp.zeros((local_kv, group_size, span_len), jnp.float32),
        jnp.zeros((local_kv, group_size, span_len, head_dim), jnp.float32),
    )
    block_total = cache_keys.shape[0] // block_len
    running = lax.fori_loop(0, block_total, sweep_block, running)
    query_rows = jnp.arange(span_len, dtype=jnp.int32)[:, None]
    key_rows = first_new + jnp.arange(row_count, dtype=jnp.int32)[None, :]
    maxima, totals, weighted = attend(
        running, query_low, new_key_rot, my_values, (key_rows <= query_rows)[None, None]
    )
    global_max = lax.pmax(maxima, "seq")
    rescale = jnp.exp(maxima - global_max)
    totals, weighted = lax.psum((totals * rescale, weighted * rescale[..., None]), "seq")
    attended = (
        (weighted / totals[..., None])
        .transpose(2, 0, 1, 3)
        .reshape(span_len, local_kv * group_size * head_dim)
    )
    attended = attended.astype(jnp.bfloat16)
    partial_out = jnp.dot(attended, w_out, preferred_element_type=jnp.float32)
    return lax.psum_scatter(
        partial_out.astype(jnp.bfloat16), "head", scatter_dimension=0, tiled=True
    )


def solution(mesh):
    return jax.shard_map(
        local,
        mesh=mesh,
        in_specs=(
            P(None, "seq"),
            P(None, "seq"),
            P("seq", "head"),
            P("seq", "head"),
            P("seq", "head"),
            P("head", "seq"),
            P("seq", "head", None),
            P("seq", "head", None),
            P(),
            P(),
        ),
        out_specs=P("head", "seq"),
        check_vma=False,
    )
```

profile of v0, /device:TPU:0, one launch (start us, length us, event | category | flops | bytes accessed | tf_op | source)
XLA Modules:
  0.0 316.9 jit_solution(12627172227235214225)
XLA Ops:
  6.5 0.8 mul.477
  7.3 1.1 fusion.24
  8.4 23.1 %psum.28 = f32[256]{0:T(256)S(1)} all-reduce(f32[256]{0:T(256)S(1)} %fusion.24), channel_id=1, replica_groups=mesh['seq'=8,'head'=4] {'seq'}, use_global_device_ids=true, to_apply=%region_3.0 | all-reduce | flops 256 | bytes 2048 | tf_op jit(solution)/shard_map/psum | solution.py:88
  31.5 1.4 convolution_bitcast_fusion
  33.0 1.2 copy.68
  34.3 1.4 fusion.45
  35.7 1.4 fusion.47
  37.1 1.0 copy.62
  39.0 0.7 fusion.50
  41.1 68.9 %all-reduce.3.cloned.1.call-done = f32[256,8,128]{2,1,0:T(8,128)} async-done(((f32[256,8,128]{2,1,0:T(8,128)}), f32[256,8,128]{2,1,0:T(8,128)}) %all-reduce.3.cloned.1.call-update) | async-done | bytes 1048592 | tf_op jit(solution)/shard_map/psum | solution.py:91
  110.0 1.9 multiply_subtract_fusion
  112.7 74.1 %while.20 = (s32[]{:T(128)}, f32[2,4,256]{2,1,0:T(4,128)S(1)}, f32[2,4,256]{2,1,0:T(4,128)S(1)}, f32[2,4,256,128]{3,2,1,0:T(8,128)S(1)}, s32[]{:T(128)}, /*index...) while((s32[]{:T(128)}, f32[2,4,256]{2,1,0:T(4,128)S(1)}, ...), condition=%wide.region_9.10_spmd.clone, body=%wide.region_6.9_spmd.clone.sunk | while | flops 1098071808 | bytes 68825840 | solution.py:142
  112.7 0.6 fusion.70
  113.4 1.9 constant_dynamic-slice_fusion.3
  116.0 1.9 fusion.71
  118.4 4.0 %bitcast_reduce_fusion.2 = (f32[2,4,256]{2,1,0:T(4,128)S(1)}, f32[2,1024,256,4]{2,1,3,0:T(8,128)}) fusion(pred[1024]{0:T(1024)(128)(4,1)S(1)} %fusion.70, bf16[256,2,4,128]{3,0,2,1:T(8,128)(2,1)S(1)} %get-tuple-element.465, bf16[1024,2,64]{2,0,1:T(8,128)(2,1)S(1)} %get-tuple-element.425, bf16[1024,2,64]{2,0,1:T(8,128)(2,1)S(1)} %get-tuple-element.426), kind=kOutput, calls=%fused_computation.1.clone.1 | convolution fusion | flops 542111744 | bytes 9446400 | tf_op jit(solution)/shard_map/while/body/eval_jaxpr/tgrd,kgd->grtk/dot_general | solution.py:51
  122.4 4.6 %fusion.72 = f32[2,4,256]{2,1,0:T(4,128)S(1)} fusion(f32[2,1024,256,4]{2,1,3,0:T(8,128)} %get-tuple-element.428, f32[2,4,256]{2,1,0:T(4,128)S(1)} %select_maximum_fusion.2, pred[1024]{0:T(1024)(128)(4,1)S(1)} %fusion.70), kind=kLoop, calls=%fused_computation.5.clone.1 | loop fusion | flops 8386560 | bytes 8406016 | tf_op jit(solution)/shard_map/while/body/eval_jaxpr/reduce_sum | solution.py:56
  127.1 1.2 copy-done.1
  128.3 2.9 fusion.74
  131.3 0.6 fusion.70
  131.9 1.9 constant_dynamic-slice_fusion.3
  134.5 1.9 fusion.71
  136.9 4.1 %bitcast_reduce_fusion.2 = (f32[2,4,256]{2,1,0:T(4,128)S(1)}, f32[2,1024,256,4]{2,1,3,0:T(8,128)}) fusion(pred[1024]{0:T(1024)(128)(4,1)S(1)} %fusion.70, bf16[256,2,4,128]{3,0,2,1:T(8,128)(2,1)S(1)} %get-tuple-element.465, bf16[1024,2,64]{2,0,1:T(8,128)(2,1)S(1)} %get-tuple-element.425, bf16[1024,2,64]{2,0,1:T(8,128)(2,1)S(1)} %get-tuple-element.426), kind=kOutput, calls=%fused_computation.1.clone.1 | convolution fusion | flops 542111744 | bytes 9446400 | tf_op jit(solution)/shard_map/while/body/eval_jaxpr/tgrd,kgd->grtk/dot_general | solution.py:51
  141.0 4.7 %fusion.72 = f32[2,4,256]{2,1,0:T(4,128)S(1)} fusion(f32[2,1024,256,4]{2,1,3,0:T(8,128)} %get-tuple-element.428, f32[2,4,256]{2,1,0:T(4,128)S(1)} %select_maximum_fusion.2, pred[1024]{0:T(1024)(128)(4,1)S(1)} %fusion.70), kind=kLoop, calls=%fused_computation.5.clone.1 | loop fusion | flops 8386560 | bytes 8406016 | tf_op jit(solution)/shard_map/while/body/eval_jaxpr/reduce_sum | solution.py:56
  145.7 1.2 copy-done.1
  146.9 2.9 fusion.74
  149.8 0.6 fusion.70
  150.5 1.9 constant_dynamic-slice_fusion.3
  153.1 1.9 fusion.71
  155.5 4.0 %bitcast_reduce_fusion.2 = (f32[2,4,256]{2,1,0:T(4,128)S(1)}, f32[2,1024,256,4]{2,1,3,0:T(8,128)}) fusion(pred[1024]{0:T(1024)(128)(4,1)S(1)} %fusion.70, bf16[256,2,4,128]{3,0,2,1:T(8,128)(2,1)S(1)} %get-tuple-element.465, bf16[1024,2,64]{2,0,1:T(8,128)(2,1)S(1)} %get-tuple-element.425, bf16[1024,2,64]{2,0,1:T(8,128)(2,1)S(1)} %get-tuple-element.426), kind=kOutput, calls=%fused_computation.1.clone.1 | convolution fusion | flops 542111744 | bytes 9446400 | tf_op jit(solution)/shard_map/while/body/eval_jaxpr/tgrd,kgd->grtk/dot_general | solution.py:51
  159.5 4.6 %fusion.72 = f32[2,4,256]{2,1,0:T(4,128)S(1)} fusion(f32[2,1024,256,4]{2,1,3,0:T(8,128)} %get-tuple-element.428, f32[2,4,256]{2,1,0:T(4,128)S(1)} %select_maximum_fusion.2, pred[1024]{0:T(1024)(128)(4,1)S(1)} %fusion.70), kind=kLoop, calls=%fused_computation.5.clone.1 | loop fusion | flops 8386560 | bytes 8406016 | tf_op jit(solution)/shard_map/while/body/eval_jaxpr/reduce_sum | solution.py:56
  164.2 1.2 copy-done.1
  165.4 2.9 fusion.74
  168.4 0.6 fusion.70
  169.0 1.9 constant_dynamic-slice_fusion.3
  171.6 1.9 fusion.71
  174.0 4.0 %bitcast_reduce_fusion.2 = (f32[2,4,256]{2,1,0:T(4,128)S(1)}, f32[2,1024,256,4]{2,1,3,0:T(8,128)}) fusion(pred[1024]{0:T(1024)(128)(4,1)S(1)} %fusion.70, bf16[256,2,4,128]{3,0,2,1:T(8,128)(2,1)S(1)} %get-tuple-element.465, bf16[1024,2,64]{2,0,1:T(8,128)(2,1)S(1)} %get-tuple-element.425, bf16[1024,2,64]{2,0,1:T(8,128)(2,1)S(1)} %get-tuple-element.426), kind=kOutput, calls=%fused_computation.1.clone.1 | convolution fusion | flops 542111744 | bytes 9446400 | tf_op jit(solution)/shard_map/while/body/eval_jaxpr/tgrd,kgd->grtk/dot_general | solution.py:51
  178.1 4.6 %fusion.72 = f32[2,4,256]{2,1,0:T(4,128)S(1)} fusion(f32[2,1024,256,4]{2,1,3,0:T(8,128)} %get-tuple-element.428, f32[2,4,256]{2,1,0:T(4,128)S(1)} %select_maximum_fusion.2, pred[1024]{0:T(1024)(128)(4,1)S(1)} %fusion.70), kind=kLoop, calls=%fused_computation.5.clone.1 | loop fusion | flops 8386560 | bytes 8406016 | tf_op jit(solution)/shard_map/while/body/eval_jaxpr/reduce_sum | solution.py:56
  182.7 1.2 copy-done.1
  183.9 2.9 fusion.74
  186.9 0.8 convert.18
  188.2 20.3 %pmax.7 = f32[2,4,256]{2,1,0:T(4,128)S(1)} all-reduce(f32[2,4,256]{2,1,0:T(4,128)S(1)} %max.32), channel_id=1, replica_groups=mesh['seq'=8,'head'=4] {'seq'}, use_global_device_ids=true, to_apply=%region_12.13 | all-reduce | flops 2048 | bytes 16384 | tf_op jit(solution)/shard_map/pmax | solution.py:148
  208.7 1.8 fusion.21
  210.5 18.0 %psum.31 = f32[2,4,256]{2,1,0:T(4,128)S(1)} all-reduce(f32[2,4,256]{2,1,0:T(4,128)S(1)} %bitcast.91), channel_id=1, replica_groups=mesh['seq'=8,'head'=4] {'seq'}, use_global_device_ids=true, to_apply=%region_15.16 | all-reduce | flops 2048 | bytes 16384 | tf_op jit(solution)/shard_map/psum | solution.py:150
  228.5 57.8 %all-reduce.5.cloned.1.call-done = f32[2,4,256,128]{3,2,1,0:T(8,128)} async-done(((f32[2,4,256,128]{3,2,1,0:T(8,128)}), f32[2,4,256,128]{3,2,1,0:T(8,128)}) %all-reduce.5.cloned.1.call-update) | async-done | bytes 1048592 | tf_op jit(solution)/shard_map/psum | solution.py:150
  286.4 1.6 fusion.27
  288.2 2.4 convolution_convert_fusion
  290.6 19.8 %reduce-scatter.5.cloned.1.call-done = bf16[64,512]{1,0:T(8,128)(2,1)} async-done(((bf16[256,512]{1,0:T(8,128)(2,1)}), bf16[64,512]{1,0:T(8,128)(2,1)}) %reduce-scatter.5.cloned.1.call-update) | async-done | bytes 65552 | tf_op jit(solution)/shard_map/reduce_scatter | solution.py:158
  (70 shorter events, 7.2 us)
Async XLA Ops:
  6.5 25.0 %copy-start = (bf16[512,1024]{1,0:T(8,128)(2,1)S(1)}, bf16[512,1024]{1,0:T(8,128)(2,1)}, u32[]{:S(2)}) copy-start(bf16[512,1024]{1,0:T(8,128)(2,1)} %param.14) | copy-start | bytes 3145732
  6.5 32.4 %copy-start.2 = (s32[8]{0:T(128)S(1)}, s32[8]{0:T(128)}, u32[]{:S(2)}) copy-start(s32[8]{0:T(128)} %param.20) | copy-start | bytes 100
  6.5 103.5 %all-reduce.3.cloned.1.call-start = ((), (), s32[]{:S(2)}) async-start(), calls=%async_computation.2 | async-start | bytes 2097152 | tf_op jit(solution)/shard_map/psum | solution.py:91
  34.2 152.6 %reduce-scatter.7.cloned.1.call-start = ((), (), s32[]{:S(2)}) async-start(), calls=%async_computation.5 | async-start | bytes 589824 | tf_op jit(solution)/shard_map/reduce_scatter | solution.py:92
  38.2 248.2 %all-reduce.5.cloned.1.call-start = ((), (), s32[]{:S(2)}) async-start(), calls=%async_computation.3 | async-start | bytes 2097152 | tf_op jit(solution)/shard_map/psum | solution.py:150
  122.4 5.9 %copy-start.1 = (f32[2,1024,256,4]{2,1,3,0:T(8,128)S(1)}, f32[2,1024,256,4]{2,1,3,0:T(8,128)}, u32[]{:S(2)}) copy-start(f32[2,1024,256,4]{2,1,3,0:T(8,128)} %get-tuple-element.428) | copy-start | bytes 25165828 | tf_op jit(solution)/shard_map/while
  141.0 5.9 %copy-start.1 = (f32[2,1024,256,4]{2,1,3,0:T(8,128)S(1)}, f32[2,1024,256,4]{2,1,3,0:T(8,128)}, u32[]{:S(2)}) copy-start(f32[2,1024,256,4]{2,1,3,0:T(8,128)} %get-tuple-element.428) | copy-start | bytes 25165828 | tf_op jit(solution)/shard_map/while
  159.5 5.9 %copy-start.1 = (f32[2,1024,256,4]{2,1,3,0:T(8,128)S(1)}, f32[2,1024,256,4]{2,1,3,0:T(8,128)}, u32[]{:S(2)}) copy-start(f32[2,1024,256,4]{2,1,3,0:T(8,128)} %get-tuple-element.428) | copy-start | bytes 25165828 | tf_op jit(solution)/shard_map/while
  178.0 5.8 %copy-start.1 = (f32[2,1024,256,4]{2,1,3,0:T(8,128)S(1)}, f32[2,1024,256,4]{2,1,3,0:T(8,128)}, u32[]{:S(2)}) copy-start(f32[2,1024,256,4]{2,1,3,0:T(8,128)} %get-tuple-element.428) | copy-start | bytes 25165828 | tf_op jit(solution)/shard_map/while
  210.5 99.9 %reduce-scatter.5.cloned.1.call-start = ((), (), s32[]{:S(2)}) async-start(), calls=%async_computation.4 | async-start | bytes 327680 | tf_op jit(solution)/shard_map/reduce_scatter | solution.py:158
Sparse Core Ops, SparseCore 0:
  34.4 75.6 all-reduce.2
  113.4 62.1 reduce-scatter.6
  210.6 75.7 all-reduce.4
  290.7 19.6 reduce-scatter.4
where the time goes:
time: 318 us; the launch traced here: 317 us
  waiting for transfers between devices  147 us (46%)
  blocking collectives  61.5 us (19%)
  other arithmetic  41.5 us (13%)
  matrix products  36.7 us (12%)
  local copies, waits for them, and re-layouts  15.5 us (5%)
  between operations  14.7 us (5%)
    psum x1, waiting for transfers between devices, local(): lax.psum(jnp.dot(normed, w_query, preferred_element_type=jnp.float32), 's...  68.9 us
    psum x1, waiting for transfers between devices, local(): lax.psum((totals * rescale, weighted * rescale[..., None]), 'seq')  57.8 us
    psum x1, blocking collectives, local(): square_sums = lax.psum(jnp.sum(input_f32 * input_f32, axis=1), 'seq')  23.1 us
    pmax x1, blocking collectives, local(): global_max = lax.pmax(maxima, 'seq')  20.3 us
    reduce_scatter x1, waiting for transfers between devices, local(): lax.psum_scatter(partial_out.astype(jnp.bfloat16), 'head', scatter_dimens...  19.8 us
    reduce_sum x5, other arithmetic, attend(): totals = totals * rescale + jnp.sum(probability, axis=-1)  18.7 us
    psum x1, blocking collectives, local(): lax.psum((totals * rescale, weighted * rescale[..., None]), 'seq')  18 us
    dot_general x5, matrix products, attend(): jnp.einsum('tgrd,kgd->grtk', queries, key_block, preferred_element_type=j...  16.5 us
  transfers between devices with their start and end apart: 4, of which 3 were waited for; matrix products, arithmetic and copies ran while one was open for 24% of the time, Pallas kernels for 0%

commit v1 on v0

--- a/solution.py
+++ b/solution.py
@@ -88,7 +88,9 @@
     square_sums = lax.psum(jnp.sum(input_f32 * input_f32, axis=1), "seq")
     inv_rms = lax.rsqrt(square_sums[:, None] / D + epsilon)
     normed = (input_f32 * inv_rms * norm_gain.astype(jnp.float32)).astype(jnp.bfloat16)
-    queries = lax.psum(jnp.dot(normed, w_query, preferred_element_type=jnp.float32), "seq")
+    queries = jnp.sum(
+        lax.all_gather(jnp.dot(normed, w_query, preferred_element_type=jnp.float32), "seq"), axis=0
+    )
     kv_own = lax.psum_scatter(
         jnp.concatenate(
             [

time: 318 us -> 439 us (1.38)
  waiting for transfers between devices: 147 us -> 256 us
  local copies, waits for them, and re-layouts: 15.5 us -> 21 us
  other arithmetic: 41.5 us -> 46.8 us
    all_gather x0 -> x1, waiting for transfers between devices: none -> 125 us  [local(): lax.all_gather(jnp.dot(normed, w_query, preferred_element_type=jnp.float3...]
    psum x1 -> x0, waiting for transfers between devices: 68.9 us -> none  [local(): lax.psum(jnp.dot(normed, w_query, preferred_element_type=jnp.float32), 's...]
    reduce_scatter x1, waiting for transfers between devices: 0.02 us -> 54.3 us  [local(): lax.psum_scatter(jnp.concatenate([jnp.dot(normed, w_key, preferred_elemen...]
    while x12 -> x28, local copies, waits for them, and re-layouts: 4.73 us -> 8.88 us
  transfers between devices with their start and end apart: 4 -> 4, of which waited for: 3 -> 4; matrix products, arithmetic and copies ran while one was open for 24% -> 1% of each run, Pallas kernels for 0% -> 0%
where the time goes in v1:
time: 439 us; the launch traced here: 438 us
  waiting for transfers between devices  256 us (58%)
  blocking collectives  60.6 us (14%)
  other arithmetic  46.8 us (11%)
  matrix products  38.5 us (9%)
  local copies, waits for them, and re-layouts  21 us (5%)
  between operations  14.5 us (3%)
    all_gather x1, waiting for transfers between devices, local(): lax.all_gather(jnp.dot(normed, w_query, preferred_element_type=jnp.float3...  125 us
    psum x1, waiting for transfers between devices, local(): lax.psum((totals * rescale, weighted * rescale[..., None]), 'seq')  57.1 us
    reduce_scatter x1, waiting for transfers between devices, local(): lax.psum_scatter(jnp.concatenate([jnp.dot(normed, w_key, preferred_elemen...  54.3 us
    psum x1, blocking collectives, local(): square_sums = lax.psum(jnp.sum(input_f32 * input_f32, axis=1), 'seq')  23.1 us
    reduce_scatter x1, waiting for transfers between devices, local(): lax.psum_scatter(partial_out.astype(jnp.bfloat16), 'head', scatter_dimens...  19.8 us
    pmax x1, blocking collectives, local(): global_max = lax.pmax(maxima, 'seq')  18.7 us
    psum x1, blocking collectives, local(): lax.psum((totals * rescale, weighted * rescale[..., None]), 'seq')  18.7 us
    reduce_sum x5, other arithmetic, attend(): totals = totals * rescale + jnp.sum(probability, axis=-1)  18.6 us
  transfers between devices with their start and end apart: 4, of which 4 were waited for; matrix products, arithmetic and copies ran while one was open for 1% of the time, Pallas kernels for 0%

profile of v1, /device:TPU:0, one launch (start us, length us, event | category | flops | bytes accessed | tf_op | source)
XLA Modules:
  0.0 437.9 jit_solution(14526152249112623079)
XLA Ops:
  7.3 1.1 fusion.24
  8.4 23.1 %psum.21 = f32[256]{0:T(256)S(1)} all-reduce(f32[256]{0:T(256)S(1)} %fusion.24), channel_id=1, replica_groups=mesh['seq'=8,'head'=4] {'seq'}, use_global_device_ids=true, to_apply=%region_3.0 | all-reduce | flops 256 | bytes 2048 | tf_op jit(solution)/shard_map/psum | solution.py:88
  31.5 1.4 fusion.45
  32.9 1.4 fusion.47
  35.5 2.4 fusion.49
  38.7 1.4 fusion.51
  41.2 54.3 %reduce-scatter.7.cloned.1.call-done = f32[32,512]{1,0:T(8,128)} async-done(((f32[256,512]{1,0:T(8,128)}), f32[32,512]{1,0:T(8,128)}) %reduce-scatter.7.cloned.1.call-update) | async-done | bytes 65552 | tf_op jit(solution)/shard_map/reduce_scatter | solution.py:94
  96.5 124.6 %all-gather.3.cloned.1.call-done = f32[2048,1024]{1,0:T(8,128)} async-done(((f32[256,1024]{1,0:T(8,128)}), f32[2048,1024]{1,0:T(8,128)}) %all-gather.3.cloned.1.call-update) | async-done | bytes 8388624 | tf_op jit(solution)/shard_map/all_gather | solution.py:92
  221.2 4.4 reduce_sum.73
  226.8 1.4 copy.48
  228.2 1.3 copy.47
  229.5 1.6 fusion.23
  231.1 78.3 %while.20 = (s32[]{:T(128)}, f32[2,4,256]{2,1,0:T(4,128)S(1)}, f32[2,4,256]{2,1,0:T(4,128)S(1)}, f32[2,4,256,128]{3,2,1,0:T(8,128)}, s32[]{:T(128)}, /*index=5*/...) while((s32[]{:T(128)}, f32[2,4,256]{2,1,0:T(4,128)S(1)}, ...), condition=%wide.region_9.10_spmd.clone, body=%wide.region_6.9_spmd.clone.sunk | while | flops 1098071808 | bytes 77214504 | solution.py:144
  231.7 1.9 constant_dynamic-slice_fusion.3
  234.4 1.9 fusion.72
  236.8 4.0 bitcast_reduce_fusion.2
  240.9 4.6 %fusion.73 = f32[2,4,256]{2,1,0:T(4,128)S(1)} fusion(f32[2,1024,256,4]{2,1,3,0:T(8,128)} %get-tuple-element.428, f32[2,4,256]{2,1,0:T(4,128)S(1)} %select_maximum_fusion.2, pred[1024]{0:T(1024)(128)(4,1)S(1)} %fusion.71), kind=kLoop, calls=%fused_computation.5.clone.1 | loop fusion | flops 8386560 | bytes 8406016 | tf_op jit(solution)/shard_map/while/body/eval_jaxpr/reduce_sum | solution.py:56
  245.5 1.1 copy-done.1
  246.7 2.9 fusion.75
  249.6 1.1 copy-done.3
  251.3 1.9 constant_dynamic-slice_fusion.3
  254.0 1.9 fusion.72
  256.4 4.0 bitcast_reduce_fusion.2
  260.5 4.6 %fusion.73 = f32[2,4,256]{2,1,0:T(4,128)S(1)} fusion(f32[2,1024,256,4]{2,1,3,0:T(8,128)} %get-tuple-element.428, f32[2,4,256]{2,1,0:T(4,128)S(1)} %select_maximum_fusion.2, pred[1024]{0:T(1024)(128)(4,1)S(1)} %fusion.71), kind=kLoop, calls=%fused_computation.5.clone.1 | loop fusion | flops 8386560 | bytes 8406016 | tf_op jit(solution)/shard_map/while/body/eval_jaxpr/reduce_sum | solution.py:56
  265.1 1.1 copy-done.1
  266.3 2.9 fusion.75
  269.2 1.1 copy-done.3
  270.9 1.9 constant_dynamic-slice_fusion.3
  273.6 1.9 fusion.72
  276.0 4.0 bitcast_reduce_fusion.2
  280.0 4.6 %fusion.73 = f32[2,4,256]{2,1,0:T(4,128)S(1)} fusion(f32[2,1024,256,4]{2,1,3,0:T(8,128)} %get-tuple-element.428, f32[2,4,256]{2,1,0:T(4,128)S(1)} %select_maximum_fusion.2, pred[1024]{0:T(1024)(128)(4,1)S(1)} %fusion.71), kind=kLoop, calls=%fused_computation.5.clone.1 | loop fusion | flops 8386560 | bytes 8406016 | tf_op jit(solution)/shard_map/while/body/eval_jaxpr/reduce_sum | solution.py:56
  284.7 1.1 copy-done.1
  285.9 2.9 fusion.75
  288.8 1.1 copy-done.3
  290.5 1.9 constant_dynamic-slice_fusion.3
  293.2 1.9 fusion.72
  295.6 4.0 bitcast_reduce_fusion.2
  299.6 4.6 %fusion.73 = f32[2,4,256]{2,1,0:T(4,128)S(1)} fusion(f32[2,1024,256,4]{2,1,3,0:T(8,128)} %get-tuple-element.428, f32[2,4,256]{2,1,0:T(4,128)S(1)} %select_maximum_fusion.2, pred[1024]{0:T(1024)(128)(4,1)S(1)} %fusion.71), kind=kLoop, calls=%fused_computation.5.clone.1 | loop fusion | flops 8386560 | bytes 8406016 | tf_op jit(solution)/shard_map/while/body/eval_jaxpr/reduce_sum | solution.py:56
  304.3 1.1 copy-done.1
  305.4 2.9 fusion.75
  308.4 1.1 copy-done.3
  309.8 18.7 %pmax.7 = f32[2,4,256]{2,1,0:T(4,128)S(1)} all-reduce(f32[2,4,256]{2,1,0:T(4,128)S(1)} %max.32), channel_id=1, replica_groups=mesh['seq'=8,'head'=4] {'seq'}, use_global_device_ids=true, to_apply=%region_12.13 | all-reduce | flops 2048 | bytes 16384 | tf_op jit(solution)/shard_map/pmax | solution.py:150
  328.6 2.8 fusion.21
  331.5 18.7 %psum.23 = f32[2,4,256]{2,1,0:T(4,128)S(1)} all-reduce(f32[2,4,256]{2,1,0:T(4,128)S(1)} %bitcast.91), channel_id=1, replica_groups=mesh['seq'=8,'head'=4] {'seq'}, use_global_device_ids=true, to_apply=%region_15.16 | all-reduce | flops 2048 | bytes 16384 | tf_op jit(solution)/shard_map/psum | solution.py:152
  350.2 57.1 %all-reduce.2.cloned.1.call-done = f32[2,4,256,128]{3,2,1,0:T(8,128)} async-done(((f32[2,4,256,128]{3,2,1,0:T(8,128)}), f32[2,4,256,128]{3,2,1,0:T(8,128)}) %all-reduce.2.cloned.1.call-update) | async-done | bytes 1048592 | tf_op jit(solution)/shard_map/psum | solution.py:152
  407.3 1.6 fusion.27
  409.1 2.4 convolution_convert_fusion
  411.5 19.8 %reduce-scatter.5.cloned.1.call-done = bf16[64,512]{1,0:T(8,128)(2,1)} async-done(((bf16[256,512]{1,0:T(8,128)(2,1)}), bf16[64,512]{1,0:T(8,128)(2,1)}) %reduce-scatter.5.cloned.1.call-update) | async-done | bytes 65552 | tf_op jit(solution)/shard_map/reduce_scatter | solution.py:160
  (85 shorter events, 12.9 us)
Async XLA Ops:
  6.5 28.9 %copy-start = (bf16[512,1024]{1,0:T(8,128)(2,1)S(1)}, bf16[512,1024]{1,0:T(8,128)(2,1)}, u32[]{:S(2)}) copy-start(bf16[512,1024]{1,0:T(8,128)(2,1)} %param.14) | copy-start | bytes 3145732
  6.5 89.0 %reduce-scatter.7.cloned.1.call-start = ((), (), s32[]{:S(2)}) async-start(), calls=%async_computation.5 | async-start | bytes 589824 | tf_op jit(solution)/shard_map/reduce_scatter | solution.py:94
  35.4 185.7 %all-gather.3.cloned.1.call-start = ((), (), s32[]{:S(2)}) async-start(), calls=%async_computation.4 | async-start | bytes 9437184 | tf_op jit(solution)/shard_map/all_gather | solution.py:92
  37.9 369.4 %all-reduce.2.cloned.1.call-start = ((), (), s32[]{:S(2)}) async-start(), calls=%async_computation.2 | async-start | bytes 2097152 | tf_op jit(solution)/shard_map/psum | solution.py:152
  236.8 8.7 %copy-start.2 = (f32[2,4,256,128]{3,2,1,0:T(8,128)S(1)}, f32[2,4,256,128]{3,2,1,0:T(8,128)}, u32[]{:S(2)}) copy-start(f32[2,4,256,128]{3,2,1,0:T(8,128)} %get-tuple-element.448) | copy-start | bytes 3145732 | tf_op jit(solution)/shard_map/while
  240.9 5.8 %copy-start.1 = (f32[2,1024,256,4]{2,1,3,0:T(8,128)S(1)}, f32[2,1024,256,4]{2,1,3,0:T(8,128)}, u32[]{:S(2)}) copy-start(f32[2,1024,256,4]{2,1,3,0:T(8,128)} %get-tuple-element.428) | copy-start | bytes 25165828 | tf_op jit(solution)/shard_map/while
  249.6 1.1 copy-start.3
  256.4 8.7 %copy-start.2 = (f32[2,4,256,128]{3,2,1,0:T(8,128)S(1)}, f32[2,4,256,128]{3,2,1,0:T(8,128)}, u32[]{:S(2)}) copy-start(f32[2,4,256,128]{3,2,1,0:T(8,128)} %get-tuple-element.448) | copy-start | bytes 3145732 | tf_op jit(solution)/shard_map/while
  260.4 5.8 %copy-start.1 = (f32[2,1024,256,4]{2,1,3,0:T(8,128)S(1)}, f32[2,1024,256,4]{2,1,3,0:T(8,128)}, u32[]{:S(2)}) copy-start(f32[2,1024,256,4]{2,1,3,0:T(8,128)} %get-tuple-element.428) | copy-start | bytes 25165828 | tf_op jit(solution)/shard_map/while
  269.2 1.1 copy-start.3
  276.0 8.7 %copy-start.2 = (f32[2,4,256,128]{3,2,1,0:T(8,128)S(1)}, f32[2,4,256,128]{3,2,1,0:T(8,128)}, u32[]{:S(2)}) copy-start(f32[2,4,256,128]{3,2,1,0:T(8,128)} %get-tuple-element.448) | copy-start | bytes 3145732 | tf_op jit(solution)/shard_map/while
  280.0 5.8 %copy-start.1 = (f32[2,1024,256,4]{2,1,3,0:T(8,128)S(1)}, f32[2,1024,256,4]{2,1,3,0:T(8,128)}, u32[]{:S(2)}) copy-start(f32[2,1024,256,4]{2,1,3,0:T(8,128)} %get-tuple-element.428) | copy-start | bytes 25165828 | tf_op jit(solution)/shard_map/while
  288.8 1.1 copy-start.3
  295.6 8.7 %copy-start.2 = (f32[2,4,256,128]{3,2,1,0:T(8,128)S(1)}, f32[2,4,256,128]{3,2,1,0:T(8,128)}, u32[]{:S(2)}) copy-start(f32[2,4,256,128]{3,2,1,0:T(8,128)} %get-tuple-element.448) | copy-start | bytes 3145732 | tf_op jit(solution)/shard_map/while
  299.6 5.8 %copy-start.1 = (f32[2,1024,256,4]{2,1,3,0:T(8,128)S(1)}, f32[2,1024,256,4]{2,1,3,0:T(8,128)}, u32[]{:S(2)}) copy-start(f32[2,1024,256,4]{2,1,3,0:T(8,128)} %get-tuple-element.428) | copy-start | bytes 25165828 | tf_op jit(solution)/shard_map/while
  308.4 1.1 copy-start.3
  331.4 99.9 %reduce-scatter.5.cloned.1.call-start = ((), (), s32[]{:S(2)}) async-start(), calls=%async_computation.3 | async-start | bytes 327680 | tf_op jit(solution)/shard_map/reduce_scatter | solution.py:160
Sparse Core Ops, SparseCore 0:
  35.5 59.9 reduce-scatter.6
  97.6 123.4 all-gather.2
  331.6 75.7 all-reduce.1
  411.6 19.6 reduce-scatter.4
